TPU v7x, 256 devices: a whole 4x4x8 slice. The times are simulated.
256 devices in a mesh: section: 8 (over y, core), expert: 32 (over x, z).
Axes of the slice: x: 4, y: 4, z: 8, core: 2. Of those that a mesh axis runs over, the one named last changes fastest.
Arguments:
- tokens_in: bfloat16 [8, 512, 2048], P(None, 'expert'), may hold values from -6 to 6
- expert_ids: int32 [8, 8, 512, 8], P('section'), may hold values from 0 to 31, as said below
- gate_values: float32 [8, 8, 512, 8], P('section', None, 'expert'), may hold values from 0.1 to 1
- expert_gate: bfloat16 [8, 32, 2048, 768], P('section', 'expert'), may hold values from -0.125 to 0.125
- expert_up: bfloat16 [8, 32, 2048, 768], P('section', 'expert'), may hold values from -0.125 to 0.125
- expert_down: bfloat16 [8, 32, 768, 2048], P('section', 'expert'), may hold values from -0.21875 to 0.21875
Outputs:
- layer_out: bfloat16 [8, 8, 512, 2048], P('section', None, 'expert')
Inputs may be any that keep to these rules, and one draw needn't show every extreme that they name: `expert_ids`: every row names 8 different experts. In each layer and micro-batch the 16 rows of one device (aligned blocks) name no expert more than 6 times, and one expert is named exactly 6 times by the rows of every device.
All inputs are finite; a program needn't handle non-finite values.
Results may differ from a plain program's by a relative error of at most 0.025.
Values may be sent and summed in bfloat16 or wider, within the bound.
A program may use at most 64 MiB of HBM per device.

v0:
```python
import jax
import jax.numpy as jnp
from jax import lax
from jax.experimental import pallas as pl
from jax.experimental.pallas import tpu as pltpu
from jax.sharding import PartitionSpec as P

epsilon = 1e-06
MESH = pl.DeviceIdType.MESH
STREAMS = 4
ORDER = (("spread", 0), ("expert", 3), ("finish", 6), ("combine", 4), ("route", 1))
most_rows = 6


def make_kernel(sizes, streams, order):
    nsec, nx, nz, batches, tok, topk, feat, ff, slot = sizes
    src_count = nz // streams
    width = src_count * tok
    items = batches * streams
    rows = nx * slot

    def kernel(
        tok_ref, ids_ref, gate_ref, wg_hbm, wu_hbm, wd_hbm, out_ref,
        wg, wu, wd, hbuf, ag, sel, xs, xr, hid, ys, yr, ps, zr, gbuf,
        w_sem, h_sem, hs_sem, g_sem, gs_sem,
        z1_sem, z1s_sem, x1_sem, x1s_sem, x2_sem, x2s_sem, z2_sem, z2s_sem,
    ):
        sec = lax.axis_index("section")
        me = lax.axis_index("expert")
        x = me // nz
        z = me % nz
        my_q = z % streams
        my_i = z // streams

        def dev(xx, zz):
            return (sec, xx * nz + zz)

        def remote(src, dst, ssem, rsem, where):
            return pltpu.make_async_remote_copy(
                src_ref=src, dst_ref=dst, send_sem=ssem, recv_sem=rsem,
                device_id=where, device_id_type=MESH,
            )

        z_peers = [(z + d) % nz for d in (4, 3, 5, 2, 6, 1, 7)]
        x_peers = [(x + d) % nx for d in (2, 1, 3)]
        following = (lax.rem(sec + 1, nsec), me)
        preceding = (lax.rem(sec + nsec - 1, nsec), me)
        everyone = [dev(x, zz) for zz in z_peers] + [dev(xx, z) for xx in x_peers]
        everyone += [following, preceding]
        barrier = pltpu.get_barrier_semaphore()

        weights = [
            pltpu.make_async_copy(a, b, w_sem.at[k])
            for k, (a, b) in enumerate(((wg_hbm, wg), (wu_hbm, wu), (wd_hbm, wd)))
        ]
        first = pltpu.make_async_copy(tok_ref, hbuf, h_sem.at[batches])

        @pl.when(sec == 0)
        def _():
            first.start()

        for copy in weights:
            copy.start()
        for peer in everyone:
            pl.semaphore_signal(barrier, inc=1, device_id=peer, device_id_type=MESH)
        gbuf[z] = gate_ref[...]
        pl.semaphore_wait(barrier, len(everyone))

        @pl.when(sec == 0)
        def _():
            first.wait()

        def split(j):
            return lax.div(j, streams), lax.rem(j, streams)

        def block(i):
            return pl.ds(pl.multiple_of(i * tok, tok), tok)

        def slots(i):
            return pl.ds(pl.multiple_of(i * slot, 8), slot)

        def spread(j):
            m, q = split(j)

            @pl.when(q == my_q)
            def _():
                @pl.when(sec > 0)
                def _():
                    remote(out_ref.at[m], hbuf.at[m], hs_sem.at[m], h_sem.at[m], following).wait_recv()

                widened = hbuf[m].astype(jnp.float32)
                inverse = lax.rsqrt(jnp.mean(widened * widened, axis=-1, keepdims=True) + epsilon)
                ag[j, block(my_i), :] = (widened * inverse).astype(jnp.bfloat16)
                mine = ag.at[j, block(my_i)]
                for zz in z_peers:
                    remote(mine, mine, z1s_sem.at[j], z1_sem.at[j], dev(x, zz)).start()

            @pl.when(j == 0)
            def _():
                for zz in z_peers:
                    remote(gbuf.at[z], gbuf.at[z], gs_sem, g_sem, dev(x, zz)).start()

        def wait_blocks(j, q, sem, buf, own):
            count = src_count - own

            @pl.when((q == my_q) if own else (q != my_q))
            def _():
                part = buf.at[j, pl.ds(0, count * tok)]
                remote(part, part, sem.at[j], sem.at[j], following).wait_recv()

        def route(j):
            m, q = split(j)
            for own in (0, 1):
                if own < src_count and (own == 1 or streams > 1):
                    wait_blocks(j, q, z1_sem, ag, own)
            ids = ids_ref[j]
            picked = [jnp.where(ids == xx * nz + z, 1.0, 0.0).astype(jnp.float32) for xx in range(nx)]
            masks = jnp.concatenate(picked, axis=0)
            r_id = lax.broadcasted_iota(jnp.int32, (width, width), 0)
            c_id = lax.broadcasted_iota(jnp.int32, (width, width), 1)
            earlier = jnp.where(r_id < c_id, 1.0, 0.0).astype(jnp.bfloat16)
            ahead = jnp.dot(masks.astype(jnp.bfloat16), earlier, preferred_element_type=jnp.float32)
            slot_id = lax.broadcasted_iota(jnp.int32, (slot, width), 0).astype(jnp.float32)
            parts = []
            for xx in range(nx):
                named = jnp.sum(picked[xx], axis=0, keepdims=True)
                rank = jnp.sum(ahead[topk * xx : topk * xx + topk], axis=0, keepdims=True)
                parts.append(jnp.where(slot_id == rank, named, 0.0))
            chosen = jnp.concatenate(parts, axis=0).astype(jnp.bfloat16)
            sel[j] = chosen
            xs[j] = jnp.dot(chosen, ag[j], preferred_element_type=jnp.float32).astype(jnp.bfloat16)
            for xx in x_peers:
                remote(
                    xs.at[j, slots(xx)], xr.at[j, slots(x)], x1s_sem.at[j], x1_sem.at[j], dev(xx, z)
                ).start()
            xr[j, slots(x), :] = xs[j, slots(x), :]

        def expert(j):
            part = xr.at[j, pl.ds(0, (nx - 1) * slot)]
            remote(part, part, x1s_sem.at[j], x1_sem.at[j], following).wait_recv()

            @pl.when(j == 0)
            def _():
                for copy in weights:
                    copy.wait()

            gate = jnp.dot(xr[j], wg[...], preferred_element_type=jnp.float32)
            up = jnp.dot(xr[j], wu[...], preferred_element_type=jnp.float32)
            hid[...] = (gate / (1.0 + jnp.exp(-gate)) * up).astype(jnp.bfloat16)
            ys[j] = jnp.dot(hid[...], wd[...], preferred_element_type=jnp.float32).astype(jnp.bfloat16)
            for xx in x_peers:
                remote(
                    ys.at[j, slots(xx)], yr.at[j, slots(x)], x2s_sem.at[j], x2_sem.at[j], dev(xx, z)
                ).start()
            yr[j, slots(x), :] = ys[j, slots(x), :]

        def combine(j):
            m, q = split(j)

            @pl.when(j == 0)
            def _():
                part = gbuf.at[pl.ds(0, nz - 1)]
                remote(part, part, gs_sem, g_sem, following).wait_recv()

            part = yr.at[j, pl.ds(0, (nx - 1) * slot)]
            remote(part, part, x2s_sem.at[j], x2_sem.at[j], following).wait_recv()
            ids = ids_ref[j]
            gates = gbuf[q, m]
            for i in range(1, src_count):
                gates = gates + gbuf[i * streams + q, m]
            high, low = [], []
            for xx in range(nx):
                weight = jnp.sum(jnp.where(ids == xx * nz + z, gates, 0.0), axis=0, keepdims=True)
                top = weight.astype(jnp.bfloat16).astype(jnp.float32)
                high.append(jnp.broadcast_to(top, (slot, width)))
                low.append(jnp.broadcast_to(weight - top, (slot, width)))
            chosen = sel[j].astype(jnp.float32)
            high = (chosen * jnp.concatenate(high, axis=0)).astype(jnp.bfloat16)
            low = (chosen * jnp.concatenate(low, axis=0)).astype(jnp.bfloat16)
            dims = (((0,), (0,)), ((), ()))
            total = lax.dot_general(high, yr[j], dims, preferred_element_type=jnp.float32)
            total = total + lax.dot_general(low, yr[j], dims, preferred_element_type=jnp.float32)
            ps[j] = total.astype(jnp.bfloat16)
            for i in range(src_count):
                target = i * streams + q

                @pl.when(target != z)
                def _():
                    remote(
                        ps.at[j, pl.ds(i * tok, tok)], zr.at[m, block(z)],
                        z2s_sem.at[j], z2_sem.at[m], dev(x, target),
                    ).start()

                @pl.when(target == z)
                def _():
                    zr[m, block(z), :] = ps[j, pl.ds(i * tok, tok), :]

        def finish(j):
            m, q = split(j)

            @pl.when(q == my_q)
            def _():
                part = zr.at[m, pl.ds(0, (nz - 1) * tok)]
                remote(part, part, z2_sem.at[m], z2_sem.at[m], following).wait_recv()
                total = zr[m, pl.ds(0, tok), :].astype(jnp.float32)
                for i in range(1, nz):
                    total = total + zr[m, pl.ds(i * tok, tok), :].astype(jnp.float32)
                out_ref[m] = (hbuf[m].astype(jnp.float32) + total).astype(jnp.bfloat16)

                @pl.when(sec < nsec - 1)
                def _():
                    remote(out_ref.at[m], hbuf.at[m], hs_sem.at[m], h_sem.at[m], following).start()

        stages = dict(spread=spread, route=route, expert=expert, combine=combine, finish=finish)
        last_lag = max(lag for _, lag in order)

        def one_step(i, carry):
            for name, lag in order:

                @pl.when((i >= lag) & (i < items + lag))
                def _():
                    stages[name](i - lag)

            return carry

        lax.fori_loop(0, items + last_lag, one_step, 0)

        def drain(j, carry):
            m, q = split(j)
            three = xs.at[j, pl.ds(0, (nx - 1) * slot)]
            remote(three, three, x1s_sem.at[j], x1_sem.at[j], following).wait_send()
            remote(three, three, x2s_sem.at[j], x2_sem.at[j], following).wait_send()
            few = ag.at[j, pl.ds(0, (src_count - 1) * tok)]
            many = ag.at[j]

            @pl.when(q == my_q)
            def _():
                seven = zr.at[m, pl.ds(0, (nz - 1) * tok)]
                remote(seven, seven, z1s_sem.at[j], z1_sem.at[j], following).wait_send()
                if src_count > 1:
                    remote(few, few, z2s_sem.at[j], z2_sem.at[m], following).wait_send()

                @pl.when(sec < nsec - 1)
                def _():
                    remote(out_ref.at[m], hbuf.at[m], hs_sem.at[m], h_sem.at[m], following).wait_send()

            @pl.when(q != my_q)
            def _():
                remote(many, many, z2s_sem.at[j], z2_sem.at[m], following).wait_send()

            return carry

        lax.fori_loop(0, items, drain, 0)
        seven = gbuf.at[pl.ds(0, nz - 1)]
        remote(seven, seven, gs_sem, g_sem, following).wait_send()

    bf16 = jnp.bfloat16
    dma = pltpu.SemaphoreType.DMA
    scratch = [
        pltpu.VMEM((feat, ff), bf16), pltpu.VMEM((feat, ff), bf16), pltpu.VMEM((ff, feat), bf16),
        pltpu.VMEM((batches, tok, feat), bf16),
        pltpu.VMEM((items, width, feat), bf16),
        pltpu.VMEM((items, rows, width), bf16),
        pltpu.VMEM((items, rows, feat), bf16), pltpu.VMEM((items, rows, feat), bf16),
        pltpu.VMEM((rows, ff), bf16),
        pltpu.VMEM((items, rows, feat), bf16), pltpu.VMEM((items, rows, feat), bf16),
        pltpu.VMEM((items, width, feat), bf16),
        pltpu.VMEM((batches, nz * tok, feat), bf16),
        pltpu.VMEM((nz, batches, topk, width), jnp.float32),
        dma((3,)), dma((batches + 1,)), dma((batches,)), dma, dma,
        dma((items,)), dma((items,)), dma((items,)), dma((items,)),
        dma((items,)), dma((items,)), dma((batches,)), dma((items,)),
    ]
    return kernel, scratch


def solution(mesh, streams=STREAMS, order=ORDER):
    nsec = mesh.shape["section"]
    nx, nz = 4, mesh.shape["expert"] // 4

    def body(tokens_in, expert_ids, gate_values, expert_gate, expert_up, expert_down):
        batches, tok, feat = tokens_in.shape
        topk = expert_ids.shape[3]
        ff = expert_gate.shape[3]
        src_count = nz // streams
        width = src_count * tok
        items = batches * streams
        slot = -(-src_count * most_rows // 8) * 8
        me = lax.axis_index("expert")
        ids = lax.dynamic_slice_in_dim(expert_ids[0], (me // nz) * (nz * tok), nz * tok, 1)
        ids = ids.reshape(batches, src_count, streams, tok, topk)
        ids = ids.transpose(0, 2, 4, 1, 3).reshape(items, topk, width)
        gates = jnp.swapaxes(gate_values[0], 1, 2)
        lanes = jnp.arange(width, dtype=jnp.int32) // tok
        gates = jnp.where(lanes == (me % nz) // streams, jnp.tile(gates, (1, 1, src_count)), 0.0)
        sizes = (nsec, nx, nz, batches, tok, topk, feat, ff, slot)
        kernel, scratch = make_kernel(sizes, streams, order)
        vmem = pl.BlockSpec(memory_space=pltpu.VMEM)
        hbm = pl.BlockSpec(memory_space=pl.ANY)
        out = pl.pallas_call(
            kernel,
            out_shape=jax.ShapeDtypeStruct((batches, tok, feat), jnp.bfloat16),
            in_specs=[hbm, vmem, vmem, hbm, hbm, hbm],
            out_specs=vmem,
            scratch_shapes=scratch,
            compiler_params=pltpu.CompilerParams(
                collective_id=0, has_side_effects=True, vmem_limit_bytes=67000000
            ),
            name="relay",
        )(tokens_in, ids, gates, expert_gate[0, 0], expert_up[0, 0], expert_down[0, 0])
        return out[None]

    return jax.shard_map(
        body,
        mesh=mesh,
        in_specs=(
            P(None, "expert", None),
            P("section", None, None, None),
            P("section", None, "expert", None),
            P("section", "expert", None, None),
            P("section", "expert", None, None),
            P("section", "expert", None, None),
        ),
        out_specs=P("section", None, "expert", None),
        check_vma=False,
    )
```

profile of v0, /device:TPU:121, one launch (start us, length us, event | category | flops | bytes accessed | tf_op | source)
XLA Modules:
  0.0 484.5 jit_solution(16264358606758612043)
XLA Ops:
  0.0 0.8 constant_dynamic-slice_fusion
  0.8 0.8 tile.4
  1.6 0.1 tile.10
  1.7 0.6 broadcast_select_fusion.gate_ref
  2.3 0.2 reshape.12
  2.5 0.1 copy.7
  2.6 0.8 reshape.13.ids_ref
  3.5 479.1 %relay.1 = bf16[8,16,2048]{2,1,0:T(8,128)(2,1)} custom-call(bf16[8,16,2048]{2,1,0:T(8,128)(2,1)} %tok_ref.1, s32[32,8,32]{2,1,0:T(8,128)} %reshape.13.ids_ref, f32[8,8,32]{2,1,0:T(8,128)} %broadcast_select_fusion.gate_ref, bf16[2048,768]{1,0:T(8,128)(2,1)} %bitcast.12, bf16[2048,768]{1,0:T(8,128)(2,1)} %bitcast.13, bf16[768,2048]{1,0:T(8,128)(2,1)} %bitcast.14), custom_call_target="tpu_custom_call" | custom-call | tf_op jit(solution)/shard_map/relay/pallas_call | solution.py:300
  482.6 1.9 copy.9
  (1 shorter events, 0.0 us)
where the time goes:
time: 485 us; the launch traced here: 484 us
  Pallas kernels  479 us (99%)
    pallas_call x1, Pallas kernels, body(): pl.pallas_call(kernel, out_shape=jax.ShapeDtypeStruct((batches, tok, feat...  479 us

commit v1 on v0

--- a/solution.py
+++ b/solution.py
@@ -8,7 +8,7 @@
 epsilon = 1e-06
 MESH = pl.DeviceIdType.MESH
 STREAMS = 4
-ORDER = (("spread", 0), ("expert", 3), ("finish", 6), ("combine", 4), ("route", 1))
+ORDER = (("spread", 0), ("expert", 3), ("combine", 4), ("route", 1))
 most_rows = 6
 
 
@@ -21,8 +21,8 @@
 
     def kernel(
         tok_ref, ids_ref, gate_ref, wg_hbm, wu_hbm, wd_hbm, out_ref,
-        wg, wu, wd, hbuf, ag, sel, xs, xr, hid, ys, yr, ps, zr, gbuf,
-        w_sem, h_sem, hs_sem, g_sem, gs_sem,
+        wg, wu, wd, hbuf, rbuf, ag, sel, xs, xr, hid, ys, yr, ps, zr, gbuf,
+        w_sem, h_sem, hs_sem, o_sem, os_sem, g_sem, gs_sem,
         z1_sem, z1s_sem, x1_sem, x1s_sem, x2_sem, x2s_sem, z2_sem, z2s_sem,
     ):
         sec = lax.axis_index("section")
@@ -46,7 +46,8 @@
         following = (lax.rem(sec + 1, nsec), me)
         preceding = (lax.rem(sec + nsec - 1, nsec), me)
         everyone = [dev(x, zz) for zz in z_peers] + [dev(xx, z) for xx in x_peers]
-        everyone += [following, preceding]
+        after, before = following[0], preceding[0]
+        everyone += [(ss, x * nz + zz) for ss in (after, before) for zz in range(nz)]
         barrier = pltpu.get_barrier_semaphore()
 
         weights = [
@@ -79,6 +80,20 @@
         def slots(i):
             return pl.ds(pl.multiple_of(i * slot, 8), slot)
 
+        def absorb(m):
+            remote(rbuf.at[m], rbuf.at[m], hs_sem.at[m], h_sem.at[m], following).wait_recv()
+            remote(zr.at[m], zr.at[m], z2_sem.at[m], z2_sem.at[m], following).wait_recv()
+            total = zr[m, pl.ds(0, tok), :].astype(jnp.float32)
+            for i in range(1, nz):
+                total = total + zr[m, pl.ds(i * tok, tok), :].astype(jnp.float32)
+            hbuf[m] = (rbuf[m].astype(jnp.float32) + total).astype(jnp.bfloat16)
+
+        def hand_back(m):
+            return remote(hbuf.at[m], out_ref.at[m], os_sem.at[m], o_sem.at[m], preceding)
+
+        def hand_on(m):
+            return remote(hbuf.at[m], rbuf.at[m], hs_sem.at[m], h_sem.at[m], following)
+
         def spread(j):
             m, q = split(j)
 
@@ -86,7 +101,7 @@
             def _():
                 @pl.when(sec > 0)
                 def _():
-                    remote(out_ref.at[m], hbuf.at[m], hs_sem.at[m], h_sem.at[m], following).wait_recv()
+                    absorb(m)
 
                 widened = hbuf[m].astype(jnp.float32)
                 inverse = lax.rsqrt(jnp.mean(widened * widened, axis=-1, keepdims=True) + epsilon)
@@ -94,6 +109,11 @@
                 mine = ag.at[j, block(my_i)]
                 for zz in z_peers:
                     remote(mine, mine, z1s_sem.at[j], z1_sem.at[j], dev(x, zz)).start()
+                hand_on(m).start()
+
+                @pl.when(sec > 0)
+                def _():
+                    hand_back(m).start()
 
             @pl.when(j == 0)
             def _():
@@ -182,36 +202,13 @@
             total = total + lax.dot_general(low, yr[j], dims, preferred_element_type=jnp.float32)
             ps[j] = total.astype(jnp.bfloat16)
             for i in range(src_count):
-                target = i * streams + q
-
-                @pl.when(target != z)
-                def _():
-                    remote(
-                        ps.at[j, pl.ds(i * tok, tok)], zr.at[m, block(z)],
-                        z2s_sem.at[j], z2_sem.at[m], dev(x, target),
-                    ).start()
-
-                @pl.when(target == z)
-                def _():
-                    zr[m, block(z), :] = ps[j, pl.ds(i * tok, tok), :]
-
-        def finish(j):
-            m, q = split(j)
-
-            @pl.when(q == my_q)
-            def _():
-                part = zr.at[m, pl.ds(0, (nz - 1) * tok)]
-                remote(part, part, z2_sem.at[m], z2_sem.at[m], following).wait_recv()
-                total = zr[m, pl.ds(0, tok), :].astype(jnp.float32)
-                for i in range(1, nz):
-                    total = total + zr[m, pl.ds(i * tok, tok), :].astype(jnp.float32)
-                out_ref[m] = (hbuf[m].astype(jnp.float32) + total).astype(jnp.bfloat16)
-
-                @pl.when(sec < nsec - 1)
-                def _():
-                    remote(out_ref.at[m], hbuf.at[m], hs_sem.at[m], h_sem.at[m], following).start()
-
-        stages = dict(spread=spread, route=route, expert=expert, combine=combine, finish=finish)
+                target = x * nz + i * streams + q
+                remote(
+                    ps.at[j, pl.ds(i * tok, tok)], zr.at[m, block(z)],
+                    z2s_sem.at[j], z2_sem.at[m], (after, target),
+                ).start()
+
+        stages = dict(spread=spread, route=route, expert=expert, combine=combine)
         last_lag = max(lag for _, lag in order)
 
         def one_step(i, carry):
@@ -230,35 +227,50 @@
             three = xs.at[j, pl.ds(0, (nx - 1) * slot)]
             remote(three, three, x1s_sem.at[j], x1_sem.at[j], following).wait_send()
             remote(three, three, x2s_sem.at[j], x2_sem.at[j], following).wait_send()
-            few = ag.at[j, pl.ds(0, (src_count - 1) * tok)]
             many = ag.at[j]
+            remote(many, many, z2s_sem.at[j], z2_sem.at[m], following).wait_send()
 
             @pl.when(q == my_q)
             def _():
                 seven = zr.at[m, pl.ds(0, (nz - 1) * tok)]
                 remote(seven, seven, z1s_sem.at[j], z1_sem.at[j], following).wait_send()
-                if src_count > 1:
-                    remote(few, few, z2s_sem.at[j], z2_sem.at[m], following).wait_send()
-
-                @pl.when(sec < nsec - 1)
+                hand_on(m).wait_send()
+
+                @pl.when(sec > 0)
                 def _():
-                    remote(out_ref.at[m], hbuf.at[m], hs_sem.at[m], h_sem.at[m], following).wait_send()
-
-            @pl.when(q != my_q)
-            def _():
-                remote(many, many, z2s_sem.at[j], z2_sem.at[m], following).wait_send()
+                    hand_back(m).wait_send()
 
             return carry
 
         lax.fori_loop(0, items, drain, 0)
         seven = gbuf.at[pl.ds(0, nz - 1)]
         remote(seven, seven, gs_sem, g_sem, following).wait_send()
+
+        @pl.when(sec == 0)
+        def _():
+            def close(m, carry):
+                absorb(m)
+                hand_back(m).start()
+                return carry
+
+            def closed(m, carry):
+                hand_back(m).wait_send()
+                return carry
+
+            lax.fori_loop(0, batches, close, 0)
+            lax.fori_loop(0, batches, closed, 0)
+
+        def arrived(m, carry):
+            hand_back(m).wait_recv()
+            return carry
+
+        lax.fori_loop(0, batches, arrived, 0)
 
     bf16 = jnp.bfloat16
     dma = pltpu.SemaphoreType.DMA
     scratch = [
         pltpu.VMEM((feat, ff), bf16), pltpu.VMEM((feat, ff), bf16), pltpu.VMEM((ff, feat), bf16),
-        pltpu.VMEM((batches, tok, feat), bf16),
+        pltpu.VMEM((batches, tok, feat), bf16), pltpu.VMEM((batches, tok, feat), bf16),
         pltpu.VMEM((items, width, feat), bf16),
         pltpu.VMEM((items, rows, width), bf16),
         pltpu.VMEM((items, rows, feat), bf16), pltpu.VMEM((items, rows, feat), bf16),
@@ -267,7 +279,7 @@
         pltpu.VMEM((items, width, feat), bf16),
         pltpu.VMEM((batches, nz * tok, feat), bf16),
         pltpu.VMEM((nz, batches, topk, width), jnp.float32),
-        dma((3,)), dma((batches + 1,)), dma((batches,)), dma, dma,
+        dma((3,)), dma((batches + 1,)), dma((batches,)), dma((batches,)), dma((batches,)), dma, dma,
         dma((items,)), dma((items,)), dma((items,)), dma((items,)),
         dma((items,)), dma((items,)), dma((batches,)), dma((items,)),
     ]

time: 485 us -> 478 us (0.986)
  Pallas kernels: 479 us -> 472 us
    pallas_call x1, Pallas kernels: 479 us -> 472 us  [body(): pl.pallas_call(kernel, out_shape=jax.ShapeDtypeStruct((batches, tok, feat...]
where the time goes in v1:
time: 478 us
  Pallas kernels  472 us (99%)
    pallas_call x1, Pallas kernels, body(): pl.pallas_call(kernel, out_shape=jax.ShapeDtypeStruct((batches, tok, feat...  472 us

profile of v1, /device:TPU:121, one launch (start us, length us, event | category | flops | bytes accessed | tf_op | source)
XLA Modules:
  0.0 477.7 jit_solution(3895908767131956810)
XLA Ops:
  0.0 0.8 constant_dynamic-slice_fusion
  0.8 0.8 tile.4
  1.6 0.1 tile.10
  1.7 0.6 broadcast_select_fusion.gate_ref
  2.3 0.2 reshape.12
  2.5 0.1 copy.7
  2.6 0.8 reshape.13.ids_ref
  3.5 472.4 %relay.1 = bf16[8,16,2048]{2,1,0:T(8,128)(2,1)} custom-call(bf16[8,16,2048]{2,1,0:T(8,128)(2,1)} %tok_ref.1, s32[32,8,32]{2,1,0:T(8,128)} %reshape.13.ids_ref, f32[8,8,32]{2,1,0:T(8,128)} %broadcast_select_fusion.gate_ref, bf16[2048,768]{1,0:T(8,128)(2,1)} %bitcast.12, bf16[2048,768]{1,0:T(8,128)(2,1)} %bitcast.13, bf16[768,2048]{1,0:T(8,128)(2,1)} %bitcast.14), custom_call_target="tpu_custom_call" | custom-call | tf_op jit(solution)/shard_map/relay/pallas_call | solution.py:312
  475.8 1.9 copy.9
  (1 shorter events, 0.0 us)

commit v2 on v1

--- a/solution.py
+++ b/solution.py
@@ -167,11 +167,16 @@
             gate = jnp.dot(xr[j], wg[...], preferred_element_type=jnp.float32)
             up = jnp.dot(xr[j], wu[...], preferred_element_type=jnp.float32)
             hid[...] = (gate / (1.0 + jnp.exp(-gate)) * up).astype(jnp.bfloat16)
-            ys[j] = jnp.dot(hid[...], wd[...], preferred_element_type=jnp.float32).astype(jnp.bfloat16)
-            for xx in x_peers:
-                remote(
-                    ys.at[j, slots(xx)], yr.at[j, slots(x)], x2s_sem.at[j], x2_sem.at[j], dev(xx, z)
-                ).start()
+            for first_col in (0, feat // 2):
+                cols = pl.ds(first_col, feat // 2)
+                ys[j, :, cols] = jnp.dot(
+                    hid[...], wd[:, cols], preferred_element_type=jnp.float32
+                ).astype(jnp.bfloat16)
+                for xx in x_peers:
+                    remote(
+                        ys.at[j, slots(xx), cols], yr.at[j, slots(x), cols],
+                        x2s_sem.at[j], x2_sem.at[j], dev(xx, z),
+                    ).start()
             yr[j, slots(x), :] = ys[j, slots(x), :]
 
         def combine(j):

time: 478 us -> 475 us (level)
  no operation moved by 1% of the time
where the time goes in v2:
time: 475 us; the launch traced here: 478 us
  Pallas kernels  473 us (100%)
    pallas_call x1, Pallas kernels, body(): pl.pallas_call(kernel, out_shape=jax.ShapeDtypeStruct((batches, tok, feat...  473 us

profile of v2, /device:TPU:121, one launch (start us, length us, event | category | flops | bytes accessed | tf_op | source)
XLA Modules:
  0.0 478.2 jit_solution(3261435570032230909)
XLA Ops:
  0.0 0.8 constant_dynamic-slice_fusion
  0.8 0.8 tile.4
  1.6 0.1 tile.10
  1.7 0.6 broadcast_select_fusion.gate_ref
  2.3 0.2 reshape.12
  2.5 0.1 copy.7
  2.6 0.8 reshape.13.ids_ref
  3.5 472.8 %relay.1 = bf16[8,16,2048]{2,1,0:T(8,128)(2,1)} custom-call(bf16[8,16,2048]{2,1,0:T(8,128)(2,1)} %tok_ref.1, s32[32,8,32]{2,1,0:T(8,128)} %reshape.13.ids_ref, f32[8,8,32]{2,1,0:T(8,128)} %broadcast_select_fusion.gate_ref, bf16[2048,768]{1,0:T(8,128)(2,1)} %bitcast.12, bf16[2048,768]{1,0:T(8,128)(2,1)} %bitcast.13, bf16[768,2048]{1,0:T(8,128)(2,1)} %bitcast.14), custom_call_target="tpu_custom_call" | custom-call | tf_op jit(solution)/shard_map/relay/pallas_call | solution.py:317
  476.3 1.9 copy.9
  (1 shorter events, 0.0 us)
